TPU v7x, 32 devices: a whole 2x2x4 slice. The times are simulated.
32 devices in a mesh: range: 4 (over y, core), chan: 8 (over z, x).
Axes of the slice: x: 2, y: 2, z: 4, core: 2. Of those that a mesh axis runs over, the one named last changes fastest.
Arguments:
- echoes: float32 [2, 64, 512, 1024], P(None, 'chan', None, 'range'), may hold values from -18 to 18
- chirp: float32 [2, 129], replicated, may hold values from -0.375 to 0.375
- train_mask: int32 [512, 8], P('chan', 'range'), may hold values from 0 to 1, as said below
Outputs:
- spectra: bfloat16 [2, 512, 64, 1024], P(None, 'chan', None, 'range')
- factors: float32 [512, 2, 128, 128], P('chan')
Inputs may be any that keep to these rules, and one draw needn't show every extreme that they name: `train_mask`: in each Doppler bin exactly 4 consecutive tiles are 0 and all other tiles are 1.
All inputs are finite; a program needn't handle non-finite values.
Results may differ from a plain program's by a relative error of at most 0.001.
Values sent between devices are 32-bit elements; how exact they have to be, the bound alone decides.
A program may use at most 128 MiB of HBM per device.

v0:
```python
import math
import jax
import jax.numpy as jnp
from jax import lax
from jax.sharding import PartitionSpec as P

TILE = 128
best_precision = lax.Precision.HIGHEST


def from_behind(value, axis, steps):
    count = lax.axis_size(axis)
    leading, last = (max(0, -steps), min(count, count - steps))
    return lax.ppermute(value, axis, [(source, source + steps) for source in range(leading, last)])


def from_behind_2(block, axis, distance):
    devices = range(lax.axis_size(axis))
    route = [((i - distance) % len(devices), i) for i in devices]
    return lax.ppermute(block, axis, route)


def toeplitz_rows(taps):
    tap_span = taps.shape[-1] - 1
    padded = jnp.concatenate([taps, jnp.zeros((taps.shape[0], tap_span), taps.dtype)], -1)
    tiled = jnp.tile(padded, (1, tap_span))
    return tiled[:, : 2 * tap_span * tap_span].reshape(taps.shape[0], tap_span, 2 * tap_span)


def compress(extended, taps):
    tap_span = taps.shape[-1] - 1
    lead_shape = extended.shape[:-1]
    block_count = extended.shape[-1] // tap_span - 1
    blocks = extended.reshape(lead_shape + (block_count + 1, tap_span))
    window = jnp.concatenate([blocks[..., :block_count, :], blocks[..., 1:, :]], -1)
    kernel = toeplitz_rows(taps)
    products = jnp.einsum(
        "tcpnk,sok->tscpno",
        window,
        kernel,
        precision=best_precision,
        preferred_element_type=jnp.float32,
    )
    real_part = products[0, 0] + products[1, 1]
    imag_part = products[1, 0] - products[0, 1]
    return jnp.stack([real_part, imag_part]).reshape(lead_shape + (block_count * tap_span,))


def doppler_table(bin_numbers, pulse_count):
    phase_index = (
        bin_numbers[:, None] * jnp.arange(pulse_count, dtype=jnp.int32)[None, :] % pulse_count
    )
    angles = phase_index.astype(jnp.float32) * (2.0 * math.pi / pulse_count)
    scaling = 1.0 / math.sqrt(pulse_count)
    return jnp.stack([jnp.cos(angles) * scaling, -jnp.sin(angles) * scaling])


def doppler(signal, dft_table):
    products = jnp.einsum(
        "sdp,tcpg->stdcg",
        dft_table,
        signal,
        precision=best_precision,
        preferred_element_type=jnp.float32,
    )
    return jnp.stack([products[0, 0] - products[1, 1], products[0, 1] + products[1, 0]])


def gram_block(spectra_now, spectra_next, weights, scaling):
    snapshot = jnp.concatenate([spectra_now, spectra_next], 2)
    masked = snapshot * weights[None, :, None, :]
    products = jnp.einsum(
        "tbkg,sblg->btskl",
        masked,
        snapshot,
        precision=best_precision,
        preferred_element_type=jnp.float32,
    )
    real_part = products[:, 0, 0] + products[:, 1, 1]
    imag_part = products[:, 0, 1] - products[:, 1, 0]
    return jnp.stack([real_part, imag_part], 1) * scaling


def factor(gram):
    order_size = gram.shape[-1]
    strip_size = min(16, order_size)
    columns = jnp.arange(order_size, dtype=jnp.int32)
    remaining = gram
    pieces = []
    for offset in range(0, order_size, strip_size):
        strip_rows = remaining[:, :, :strip_size, :]

        def column_step(position, carry):
            strip_now, found_rows = carry
            place = offset + position
            row_now = lax.dynamic_index_in_dim(strip_now, position, 2, keepdims=False)
            pivots = jnp.sum(jnp.where(columns == place, row_now[:, 0], 0.0), -1)
            inverse = lax.rsqrt(pivots)[:, None]
            row_real = jnp.where(columns >= place, row_now[:, 0] * inverse, 0.0)
            row_imag = jnp.where(columns > place, row_now[:, 1] * inverse, 0.0)
            coef_real = row_real[:, offset : offset + strip_size]
            coef_imag = row_imag[:, offset : offset + strip_size]
            new_real = (
                strip_now[:, 0]
                - coef_real[:, :, None] * row_real[:, None, :]
                - coef_imag[:, :, None] * row_imag[:, None, :]
            )
            new_imag = (
                strip_now[:, 1]
                - coef_real[:, :, None] * row_imag[:, None, :]
                + coef_imag[:, :, None] * row_real[:, None, :]
            )
            found_rows = lax.dynamic_update_index_in_dim(
                found_rows, jnp.stack([row_real, row_imag], 1), position, 2
            )
            return (jnp.stack([new_real, new_imag], 1), found_rows)

        strip_end, found_rows = lax.fori_loop(
            0, strip_size, column_step, (strip_rows, jnp.zeros_like(strip_rows))
        )
        pieces.append(found_rows)
        if offset + strip_size < order_size:
            tail_part = found_rows[:, :, :, offset + strip_size :]
            products = jnp.einsum(
                "nabi,ncbj->nacij",
                tail_part,
                found_rows,
                precision=best_precision,
                preferred_element_type=jnp.float32,
            )
            update_real = products[:, 0, 0] + products[:, 1, 1]
            update_imag = products[:, 0, 1] - products[:, 1, 0]
            remaining = remaining[:, :, strip_size:, :] - jnp.stack([update_real, update_imag], 1)
    return jnp.concatenate(pieces, 2)


def on_device(echoes, chirp, train_mask):
    tap_span = chirp.shape[-1] - 1
    pulses = echoes.shape[2]
    gate_count = echoes.shape[3]
    rim_gates = from_behind(echoes[..., :tap_span], "range", -1)
    compressed = compress(jnp.concatenate([echoes, rim_gates], -1), chirp)
    spectra_all = doppler(compressed, doppler_table(jnp.arange(pulses, dtype=jnp.int32), pulses))
    turned = lax.all_to_all(spectra_all, "chan", split_axis=1, concat_axis=2, tiled=True)
    edge_bin = from_behind_2(turned[:, :1], "chan", -1)
    following = jnp.concatenate([turned[:, 1:], edge_bin], 1)
    spectra_out = turned.astype(jnp.bfloat16)
    total_gates = gate_count * lax.axis_size("range")
    scaling = 1.0 / total_gates
    weights = jnp.broadcast_to(
        train_mask.astype(jnp.float32)[:, :, None], train_mask.shape + (TILE,)
    ).reshape(train_mask.shape[0], gate_count)
    partial_gram = lax.psum_scatter(
        gram_block(turned, following, weights, scaling), "range", scatter_dimension=0, tiled=True
    )
    factors = lax.all_gather(factor(partial_gram), "range", axis=0, tiled=True)
    return (spectra_out, factors)


def solution(mesh):
    return jax.shard_map(
        on_device,
        mesh=mesh,
        in_specs=(P(None, "chan", None, "range"), P(), P("chan", "range")),
        out_specs=(P(None, "chan", None, "range"), P("chan", None, None, None)),
        check_vma=False,
    )
```

profile of v0, /device:TPU:0, one launch (start us, length us, event | category | flops | bytes accessed | tf_op | source)
XLA Modules:
  0.0 662.5 jit_solution(18391180482651036311)
XLA Ops:
  7.2 8.7 %copy.189 = f32[2,8,512,256]{2,3,1,0:T(8,128)} copy(f32[2,8,512,256]{3,2,1,0:T(8,128)} %param.19) | data formatting | bytes 16777216 | tf_op args[0]
  15.9 4.8 slice.757
  22.6 4.2 negate_multiply_fusion
  26.7 3.4 collective-permute-done
  30.1 6.2 pad_maximum_fusion.8
  36.3 7.0 %fusion.104 = (f32[2,8,512,2,128]{2,4,3,1,0:T(8,128)}, f32[2,8,512,2,128]{2,4,3,1,0:T(8,128)}) fusion(f32[2,8,512,3,128]{2,4,3,1,0:T(8,128)S(1)} %bitcast.399), kind=kLoop, calls=%fused_computation.288 | loop fusion | bytes 33554432 | tf_op jit(solution)/shard_map/slice | solution.py:35
  43.3 8.7 %copy.286 = f32[2,8,512,2,128]{4,2,3,1,0:T(8,128)} copy(f32[2,8,512,2,128]{2,4,3,1,0:T(8,128)} %get-tuple-element.1093) | data formatting | bytes 16777216
  52.0 8.7 %copy.285 = f32[2,8,512,2,128]{4,2,3,1,0:T(8,128)} copy(f32[2,8,512,2,128]{2,4,3,1,0:T(8,128)} %get-tuple-element.1092) | data formatting | bytes 16777216
  60.7 21.7 %fusion.55 = f32[2,2,8,512,2,128]{3,5,4,2,0,1:T(8,128)} fusion(f32[2,8,512,2,128]{4,2,3,1,0:T(8,128)} %copy.286, f32[2,8,512,2,128]{4,2,3,1,0:T(8,128)} %copy.285, f32[1,2,128,256]{3,1,2,0:T(2,128)S(1)} %bitcast.450), kind=kOutput, calls=%fused_computation.179 | convolution fusion | flops 12889096192 | bytes 33816576 | tf_op jit(solution)/shard_map/tcpnk,sok->tscpno/dot_general | solution.py:37
  82.5 10.2 %slice_add_fusion.1 = (f32[1,1,8,512,2,128]{3,5,4,2,0,1:T(8,128)S(1)}, f32[1,1,8,512,2,128]{3,5,4,2,0,1:T(8,128)}) fusion(f32[2,2,8,512,2,128]{3,5,4,2,0,1:T(8,128)} %fusion.55), kind=kLoop, calls=%fused_computation.194 | loop fusion | flops 2097152 | bytes 25165824 | tf_op jit(solution)/shard_map/add | solution.py:44
  92.6 31.7 %fusion.56 = f32[2,2,512,8,256]{2,4,0,3,1:T(8,128)S(1)} fusion(f32[1,8,512,256]{2,3,1,0:T(8,128)} %bitcast.409, f32[1,8,512,256]{2,3,1,0:T(8,128)S(1)} %bitcast.408, f32[1,512,512]{2,1,0:T(8,128)S(1)} %get-tuple-element.1118, f32[1,512,512]{2,1,0:T(8,128)S(1)} %get-tuple-element.1119), kind=kOutput, calls=%fused_computation.180 | convolution fusion | flops 25772425216 | bytes 27262976 | tf_op jit(solution)/shard_map/sdp,tcpg->stdcg/dot_general | solution.py:59
  126.4 4.4 pad_maximum_fusion.9
  130.7 10.3 %copy.194 = f32[2,512,8,256]{3,2,0,1:T(8,128)} copy(f32[2,512,8,256]{1,3,2,0:T(8,128)} %pad_maximum_fusion.9) | data formatting | bytes 16777216 | tf_op jit(solution)/shard_map/stack | solution.py:66
  141.1 177.9 %all_to_all.18 = f32[2,512,8,256]{3,2,0,1:T(8,128)S(1)} all-to-all(f32[2,512,8,256]{3,2,0,1:T(8,128)} %copy.194), channel_id=1, replica_groups=mesh['range'=4,'chan'=8] {'chan'}, dimensions={1} | all-to-all | bytes 16777216 | tf_op jit(solution)/shard_map/all_to_all | solution.py:144
  329.2 7.6 %slice.768 = f32[2,63,64,256]{3,2,0,1:T(8,128)} slice(f32[2,64,64,256]{3,2,0,1:T(8,128)} %bitcast.402), slice={[0:2], [1:64], [0:64], [0:256]} | slice | bytes 16515072 | tf_op jit(solution)/shard_map/slice | solution.py:146
  336.8 27.5 %fusion.46 = f32[64,2,2,128,128]{3,4,1,2,0:T(8,128)} fusion(f32[2,1,64,256]{3,2,0,1:T(8,128)S(1)} %collective-permute-done.1, f32[2,63,64,256]{3,2,0,1:T(8,128)} %slice.768, f32[2,64,64,256]{3,2,0,1:T(8,128)} %bitcast.403, f32[64,256]{1,0:T(8,128)S(1)} %bitcast.452), kind=kOutput, calls=%fused_computation.169 | convolution fusion | flops 12905873408 | bytes 33619968 | tf_op jit(solution)/shard_map/tbkg,sblg->btskl/dot_general | solution.py:72
  364.3 4.2 fusion.57
  368.5 4.2 fusion.59
  375.5 8.0 %copy.365 = f32[8,8,256,128]{3,1,2,0:T(8,128)} copy(f32[8,8,256,128]{3,2,1,0:T(8,128)S(1)} %bitcast.404) | data formatting | bytes 16777216
  383.6 82.1 %reduce-scatter.5.cloned.1.call-done = f32[16,32768]{1,0:T(8,128)} async-done(((f32[64,32768]{1,0:T(8,128)}), f32[16,32768]{1,0:T(8,128)}) %reduce-scatter.5.cloned.1.call-update) | async-done | bytes 2097168
  470.2 8.8 %while.136 = (s32[]{:T(128)}, f32[16,2,16,128]{3,2,1,0:T(8,128)S(1)}, f32[16,2,16,128]{3,0,1,2:T(8,128)S(1)}, s32[]{:T(128)}) while((s32[]{:T(128)}, f32[16,2,16,128]{3,2,1,0:T(8,128)S(1)}, f32[16,2,16,128]{3,0,1,2:T(8,128)S(1)}, s32[]{:T(128)}) %tuple.404), condition=%wide.region_3.4_spmd.clone.clone, body=%wide.region_1.3_spmd.clone.clone.sunk | while | flops 345458 | bytes 1227949 | solution.py:118
  479.9 3.3 convolution_bitcast_fusion
  488.1 11.2 %while.137 = (s32[]{:T(128)}, f32[16,2,16,128]{3,2,1,0:T(8,128)S(1)}, f32[16,2,16,128]{3,0,1,2:T(8,128)S(1)}, s32[]{:T(128)}, s32[]{:T(128)}) while((s32[]{:T(128)}, f32[16,2,16,128]{3,2,1,0:T(8,128)S(1)}, f32[16,2,16,128]{3,0,1,2:T(8,128)S(1)}, s32[]{:T(128)}, s32[]{:T(128)}) %tuple.407), condition=%wide.region_6.7_spmd.clone.clone, body=%wide.region_4.6_spmd.clone.clone.sunk | while | flops 345459 | bytes 1228033 | solution.py:118
  504.7 11.2 %while.138 = (s32[]{:T(128)}, f32[16,2,16,128]{3,2,1,0:T(8,128)S(1)}, f32[16,2,16,128]{3,0,1,2:T(8,128)S(1)}, s32[]{:T(128)}, s32[]{:T(128)}) while((s32[]{:T(128)}, f32[16,2,16,128]{3,2,1,0:T(8,128)S(1)}, f32[16,2,16,128]{3,0,1,2:T(8,128)S(1)}, s32[]{:T(128)}, s32[]{:T(128)}) %tuple.410), condition=%wide.region_9.10_spmd.clone.clone, body=%wide.region_7.9_spmd.clone.clone.sunk | while | flops 345459 | bytes 1228033 | solution.py:118
  519.6 11.4 %while.139 = (s32[]{:T(128)}, f32[16,2,16,128]{3,2,1,0:T(8,128)S(1)}, f32[16,2,16,128]{3,0,1,2:T(8,128)S(1)}, s32[]{:T(128)}, s32[]{:T(128)}) while((s32[]{:T(128)}, f32[16,2,16,128]{3,2,1,0:T(8,128)S(1)}, f32[16,2,16,128]{3,0,1,2:T(8,128)S(1)}, s32[]{:T(128)}, s32[]{:T(128)}) %tuple.413), condition=%wide.region_12.13_spmd.clone.clone, body=%wide.region_10.12_spmd.clone.clone.sunk | while | flops 345459 | bytes 1228033 | solution.py:118
  534.4 11.2 %while.140 = (s32[]{:T(128)}, f32[16,2,16,128]{3,2,1,0:T(8,128)S(1)}, f32[16,2,16,128]{3,0,1,2:T(8,128)S(1)}, s32[]{:T(128)}, s32[]{:T(128)}) while((s32[]{:T(128)}, f32[16,2,16,128]{3,2,1,0:T(8,128)S(1)}, f32[16,2,16,128]{3,0,1,2:T(8,128)S(1)}, s32[]{:T(128)}, s32[]{:T(128)}) %tuple.416), condition=%wide.region_15.16_spmd.clone.clone, body=%wide.region_13.15_spmd.clone.clone.sunk | while | flops 345459 | bytes 1228033 | solution.py:118
  548.3 11.2 %while.141 = (s32[]{:T(128)}, f32[16,2,16,128]{3,2,1,0:T(8,128)S(1)}, f32[16,2,16,128]{3,0,1,2:T(8,128)S(1)}, s32[]{:T(128)}, s32[]{:T(128)}) while((s32[]{:T(128)}, f32[16,2,16,128]{3,2,1,0:T(8,128)S(1)}, f32[16,2,16,128]{3,0,1,2:T(8,128)S(1)}, s32[]{:T(128)}, s32[]{:T(128)}) %tuple.419), condition=%wide.region_18.19_spmd.clone.clone, body=%wide.region_16.18_spmd.clone.clone.sunk | while | flops 345459 | bytes 1228033 | solution.py:118
  561.9 11.2 %while.142 = (s32[]{:T(128)}, f32[16,2,16,128]{3,2,1,0:T(8,128)S(1)}, f32[16,2,16,128]{3,0,1,2:T(8,128)S(1)}, s32[]{:T(128)}, s32[]{:T(128)}) while((s32[]{:T(128)}, f32[16,2,16,128]{3,2,1,0:T(8,128)S(1)}, f32[16,2,16,128]{3,0,1,2:T(8,128)S(1)}, s32[]{:T(128)}, s32[]{:T(128)}) %tuple.422), condition=%wide.region_21.22_spmd.clone.clone, body=%wide.region_19.21_spmd.clone.clone.sunk | while | flops 345459 | bytes 1228033 | solution.py:118
  575.4 13.0 %while.143 = (s32[]{:T(128)}, f32[16,2,16,128]{3,2,1,0:T(8,128)S(1)}, f32[16,2,16,128]{3,2,1,0:T(8,128)S(1)}, s32[]{:T(128)}, s32[]{:T(128)}, /*index=5*/s32[]{:T(128)}) while((s32[]{:T(128)}, f32[16,2,16,128]{3,2,1,0:T(8,128)S(1)}, f32[16,2,16,128]{3,2,1,0:T(8,128)S(1)}, s32[]{:T(128)}, s32[]{:T(128)}, ...), condition=%wide.region_24.25_spmd.clone.clone, body=%wide.region_22.24_spmd.clone.clone.sunk | while | flops 345459 | bytes 1293577 | solution.py:118
  589.2 4.0 copy.368
  595.5 52.1 %all-gather.2.cloned.1.call-done = f32[64,2,128,128]{3,2,1,0:T(8,128)} async-done(((f32[16,2,128,128]{3,2,1,0:T(8,128)}), f32[64,2,128,128]{3,2,1,0:T(8,128)}) %all-gather.2.cloned.1.call-update) | async-done | bytes 8388624 | tf_op jit(solution)/shard_map/all_gather | solution.py:156
  647.6 7.9 %copy.476 = f32[64,2,128,128]{3,2,1,0:T(8,128)} copy(f32[64,2,128,128]{3,2,1,0:T(8,128)} %all-gather.2.cloned.1.call-done) | data formatting | bytes 16777216
  (1758 shorter events, 129.2 us)
Async XLA Ops:
  7.2 458.5 %reduce-scatter.5.cloned.1.call-start = ((), (), s32[]{:S(2)}) async-start(), calls=%async_computation.3 | async-start | bytes 10485760
  15.9 6.1 copy-start.6
  20.7 9.4 %collective-permute-start = (f32[2,8,512,128]{2,3,1,0:T(8,128)}, f32[2,8,512,128]{2,3,1,0:T(8,128)}, u32[]{:S(2)}, u32[]{:S(2)}) collective-permute-start(f32[2,8,512,128]{2,3,1,0:T(8,128)} %slice.757), channel_id=1, source_target_pairs={{8,0},{16,8},{24,16},{9,1},{17,9},{25,17},{10,2},{18,10},{26,18},{... | collective-permute-start | bytes 12582920 | tf_op jit(solution)/shard_map/ppermute | solution.py:14
  22.6 13.7 %copy-start.5 = (f32[2,32896]{1,0:T(2,128)}, f32[2,32896]{1,0:T(2,128)S(1)}, u32[]{:S(2)}) copy-start(f32[2,32896]{1,0:T(2,128)S(1)} %tile.10) | copy-start | bytes 789508
  52.0 8.7 %slice-start = ((f32[2,32896]{1,0:T(2,128)}), f32[2,32768]{1,0:T(2,128)S(1)}, s32[]{:S(2)}) async-start(f32[2,32896]{1,0:T(2,128)} %copy-done.5), calls=%async_computation.4 | async-start | bytes 524288 | tf_op jit(solution)/shard_map/slice | solution.py:27
  319.0 3.5 copy-start
  319.0 9.9 %copy-start.7 = (s32[64,2]{0,1:T(2,128)S(1)}, s32[64,2]{0,1:T(2,128)}, u32[]{:S(2)}) copy-start(s32[64,2]{0,1:T(2,128)} %param.21) | copy-start | bytes 1540
  322.5 3.3 copy-start.1
  325.8 11.0 %collective-permute-start.1 = (f32[2,1,64,256]{3,2,0,1:T(8,128)S(1)}, f32[2,1,64,256]{3,2,0,1:T(8,128)S(1)}, u32[]{:S(2)}, u32[]{:S(2)}) collective-permute-start(f32[2,1,64,256]{3,2,0,1:T(8,128)S(1)} %slice.769), channel_id=1, source_target_pairs={{1,0},{2,1},{3,2},{4,3},{5,4},{6,5},{7,6},{0,7},{9,8},{10,9},{11,1... | collective-permute-start | bytes 393224 | tf_op jit(solution)/shard_map/ppermute | solution.py:20
  383.6 264.0 %all-gather.2.cloned.1.call-start = ((), (), s32[]{:S(2)}) async-start(), calls=%async_computation.2 | async-start | bytes 10485760 | tf_op jit(solution)/shard_map/all_gather | solution.py:156
  479.9 4.4 copy-start.2
  503.5 1.1 copy-start.3
  515.9 3.5 copy-start.4
Sparse Core Ops, SparseCore 0:
  383.7 81.9 reduce-scatter.4
  589.3 58.2 all-gather.1
where the time goes:
time: 668 us; the launch traced here: 663 us
  blocking collectives  178 us (27%)
  waiting for transfers between devices  138 us (21%)
  local copies, waits for them, and re-layouts  124 us (19%)
  other arithmetic  98.7 us (15%)
  matrix products  95.1 us (14%)
  between operations  14.8 us (2%)
  loops' own time  9.7 us (1%)
    all_to_all x1, blocking collectives, on_device(): lax.all_to_all(spectra_all, 'chan', split_axis=1, concat_axis=2, tiled=True)  178 us
    unnamed x3, waiting for transfers between devices  82.1 us
    unnamed x35, local copies, waits for them, and re-layouts  57.4 us
    all_gather x1, waiting for transfers between devices, on_device(): factors = lax.all_gather(factor(partial_gram), 'range', axis=0, tiled=True)  52.1 us
    dot_general x1, matrix products, doppler(): jnp.einsum('sdp,tcpg->stdcg', dft_table, signal, precision=best_precision...  31.7 us
    dot_general x1, matrix products, gram_block(): jnp.einsum('tbkg,sblg->btskl', masked, snapshot, precision=best_precision...  27.5 us
    dot_general x1, matrix products, compress(): jnp.einsum('tcpnk,sok->tscpno', window, kernel, precision=best_precision,...  21.7 us
    select_n x256, other arithmetic, column_step(): row_real = jnp.where(columns >= place, row_now[:, 0] * inverse, 0.0)  19 us
  transfers between devices with their start and end apart: 4, of which 3 were waited for; matrix products, arithmetic and copies ran while one was open for 3% of the time, Pallas kernels for 0%

commit v1 on v0

--- a/solution.py
+++ b/solution.py
@@ -153,7 +153,13 @@
     partial_gram = lax.psum_scatter(
         gram_block(turned, following, weights, scaling), "range", scatter_dimension=0, tiled=True
     )
-    factors = lax.all_gather(factor(partial_gram), "range", axis=0, tiled=True)
+    _divide_patches = lambda my_data, lane_axis: jnp.concatenate(
+        lax.all_to_all(
+            jnp.stack([my_data for _ in range(lax.axis_size(lane_axis))]), lane_axis, 0, 0
+        ),
+        0,
+    )
+    factors = _divide_patches(factor(partial_gram), "range")
     return (spectra_out, factors)
 
 

time: 668 us -> 713 us (1.067)
  waiting for transfers between devices: 138 us -> 172 us
    all_to_all x0 -> x1, waiting for transfers between devices: none -> 86.8 us  [on_device(): lax.all_to_all(jnp.stack([my_data for _ in range(lax.axis_size(lane_axis)...]
    all_gather x1 -> x0, waiting for transfers between devices: 52.1 us -> none  [on_device(): factors = lax.all_gather(factor(partial_gram), 'range', axis=0, tiled=True)]
    unnamed x35 -> x47, local copies, waits for them, and re-layouts: 57.4 us -> 61.1 us
    unnamed x3 -> x2, waiting for transfers between devices: 82.1 us -> 82.2 us
where the time goes in v1:
time: 713 us; the launch traced here: 708 us
  blocking collectives  178 us (25%)
  waiting for transfers between devices  172 us (24%)
  local copies, waits for them, and re-layouts  128 us (18%)
  other arithmetic  98.8 us (14%)
  matrix products  96.1 us (13%)
  between operations  14.9 us (2%)
  starting transfers between devices  10.1 us (1%)
  loops' own time  9.45 us (1%)
    all_to_all x1, blocking collectives, on_device(): lax.all_to_all(spectra_all, 'chan', split_axis=1, concat_axis=2, tiled=True)  178 us
    all_to_all x1, waiting for transfers between devices, on_device(): lax.all_to_all(jnp.stack([my_data for _ in range(lax.axis_size(lane_axis)...  86.8 us
    unnamed x2, waiting for transfers between devices  82.2 us
    unnamed x47, local copies, waits for them, and re-layouts  61.1 us
    dot_general x1, matrix products, doppler(): jnp.einsum('sdp,tcpg->stdcg', dft_table, signal, precision=best_precision...  31.7 us
    dot_general x1, matrix products, gram_block(): jnp.einsum('tbkg,sblg->btskl', masked, snapshot, precision=best_precision...  27.5 us
    dot_general x1, matrix products, compress(): jnp.einsum('tcpnk,sok->tscpno', window, kernel, precision=best_precision,...  21.7 us
    select_n x256, other arithmetic, column_step(): row_real = jnp.where(columns >= place, row_now[:, 0] * inverse, 0.0)  19 us
  transfers between devices with their start and end apart: 4, of which 3 were waited for; matrix products, arithmetic and copies ran while one was open for 3% of the time, Pallas kernels for 0%

profile of v1, /device:TPU:0, one launch (start us, length us, event | category | flops | bytes accessed | tf_op | source)
XLA Modules:
  0.0 707.7 jit_solution(6341201973405232020)
XLA Ops:
  7.2 8.7 %copy.168 = f32[2,8,512,256]{2,3,1,0:T(8,128)} copy(f32[2,8,512,256]{3,2,1,0:T(8,128)} %param.19) | data formatting | bytes 16777216 | tf_op args[0]
  15.9 4.8 slice.757
  22.6 4.2 negate_multiply_fusion
  30.1 6.2 pad_maximum_fusion.8
  36.3 7.0 fusion.105
  43.3 8.8 %copy.256 = f32[2,8,512,2,128]{4,2,3,1,0:T(8,128)} copy(f32[2,8,512,2,128]{2,4,3,1,0:T(8,128)} %get-tuple-element.1093) | data formatting | bytes 16777216
  52.1 8.8 %copy.255 = f32[2,8,512,2,128]{4,2,3,1,0:T(8,128)} copy(f32[2,8,512,2,128]{2,4,3,1,0:T(8,128)} %get-tuple-element.1092) | data formatting | bytes 16777216
  60.8 21.7 %fusion.56 = f32[2,2,8,512,2,128]{3,5,4,2,0,1:T(8,128)} fusion(f32[2,8,512,2,128]{4,2,3,1,0:T(8,128)} %copy.256, f32[2,8,512,2,128]{4,2,3,1,0:T(8,128)} %copy.255, f32[1,2,128,256]{3,1,2,0:T(2,128)S(1)} %bitcast.453), kind=kOutput, calls=%fused_computation.180 | convolution fusion | flops 12889096192 | bytes 33816576 | tf_op jit(solution)/shard_map/tcpnk,sok->tscpno/dot_general | solution.py:37
  82.6 10.2 %slice_add_fusion.1 = (f32[1,1,8,512,2,128]{3,5,4,2,0,1:T(8,128)S(1)}, f32[1,1,8,512,2,128]{3,5,4,2,0,1:T(8,128)}) fusion(f32[2,2,8,512,2,128]{3,5,4,2,0,1:T(8,128)} %fusion.56), kind=kLoop, calls=%fused_computation.195 | loop fusion | flops 2097152 | bytes 25165824 | tf_op jit(solution)/shard_map/add | solution.py:44
  92.8 31.7 %fusion.57 = f32[2,2,512,8,256]{2,4,0,3,1:T(8,128)S(1)} fusion(f32[1,8,512,256]{2,3,1,0:T(8,128)} %bitcast.412, f32[1,8,512,256]{2,3,1,0:T(8,128)S(1)} %bitcast.411, f32[1,512,512]{2,1,0:T(8,128)S(1)} %get-tuple-element.1106, f32[1,512,512]{2,1,0:T(8,128)S(1)} %get-tuple-element.1107), kind=kOutput, calls=%fused_computation.181 | convolution fusion | flops 25772425216 | bytes 27262976 | tf_op jit(solution)/shard_map/sdp,tcpg->stdcg/dot_general | solution.py:59
  126.5 4.4 pad_maximum_fusion.9
  130.8 10.3 %copy.173 = f32[2,512,8,256]{3,2,0,1:T(8,128)} copy(f32[2,512,8,256]{1,3,2,0:T(8,128)} %pad_maximum_fusion.9) | data formatting | bytes 16777216 | tf_op jit(solution)/shard_map/stack | solution.py:66
  141.2 177.9 %all_to_all.23 = f32[2,512,8,256]{3,2,0,1:T(8,128)S(1)} all-to-all(f32[2,512,8,256]{3,2,0,1:T(8,128)} %copy.173), channel_id=1, replica_groups=mesh['range'=4,'chan'=8] {'chan'}, dimensions={1} | all-to-all | bytes 16777216 | tf_op jit(solution)/shard_map/all_to_all | solution.py:144
  329.3 7.6 %slice.768 = f32[2,63,64,256]{3,2,0,1:T(8,128)} slice(f32[2,64,64,256]{3,2,0,1:T(8,128)} %bitcast.404), slice={[0:2], [1:64], [0:64], [0:256]} | slice | bytes 16515072 | tf_op jit(solution)/shard_map/slice | solution.py:146
  336.9 27.5 %fusion.47 = f32[64,2,2,128,128]{3,4,1,2,0:T(8,128)} fusion(f32[2,1,64,256]{3,2,0,1:T(8,128)S(1)} %collective-permute-done.1, f32[2,63,64,256]{3,2,0,1:T(8,128)} %slice.768, f32[2,64,64,256]{3,2,0,1:T(8,128)} %bitcast.405, f32[64,256]{1,0:T(8,128)S(1)} %bitcast.455), kind=kOutput, calls=%fused_computation.170 | convolution fusion | flops 12905873408 | bytes 33619968 | tf_op jit(solution)/shard_map/tbkg,sblg->btskl/dot_general | solution.py:72
  364.4 4.2 fusion.58
  368.6 4.2 fusion.60
  375.6 8.0 %copy.321 = f32[8,8,256,128]{3,1,2,0:T(8,128)} copy(f32[8,8,256,128]{3,2,1,0:T(8,128)S(1)} %bitcast.407) | data formatting | bytes 16777216
  383.7 82.1 %reduce-scatter.5.cloned.1.call-done = f32[16,32768]{1,0:T(8,128)} async-done(((f32[64,32768]{1,0:T(8,128)}), f32[16,32768]{1,0:T(8,128)}) %reduce-scatter.5.cloned.1.call-update) | async-done | bytes 2097168
  470.4 8.8 %while.136 = (s32[]{:T(128)}, f32[16,2,16,128]{3,2,1,0:T(8,128)S(1)}, f32[16,2,16,128]{3,0,1,2:T(8,128)S(1)}, s32[]{:T(128)}) while((s32[]{:T(128)}, f32[16,2,16,128]{3,2,1,0:T(8,128)S(1)}, f32[16,2,16,128]{3,0,1,2:T(8,128)S(1)}, s32[]{:T(128)}) %tuple.398), condition=%wide.region_3.4_spmd.clone.clone, body=%wide.region_1.3_spmd.clone.clone.sunk | while | flops 345458 | bytes 1227949 | solution.py:118
  488.3 11.2 %while.137 = (s32[]{:T(128)}, f32[16,2,16,128]{3,2,1,0:T(8,128)S(1)}, f32[16,2,16,128]{3,0,1,2:T(8,128)S(1)}, s32[]{:T(128)}, s32[]{:T(128)}) while((s32[]{:T(128)}, f32[16,2,16,128]{3,2,1,0:T(8,128)S(1)}, f32[16,2,16,128]{3,0,1,2:T(8,128)S(1)}, s32[]{:T(128)}, s32[]{:T(128)}) %tuple.401), condition=%wide.region_6.7_spmd.clone.clone, body=%wide.region_4.6_spmd.clone.clone.sunk | while | flops 345459 | bytes 1228033 | solution.py:118
  504.9 11.2 %while.138 = (s32[]{:T(128)}, f32[16,2,16,128]{3,2,1,0:T(8,128)S(1)}, f32[16,2,16,128]{3,0,1,2:T(8,128)S(1)}, s32[]{:T(128)}, s32[]{:T(128)}) while((s32[]{:T(128)}, f32[16,2,16,128]{3,2,1,0:T(8,128)S(1)}, f32[16,2,16,128]{3,0,1,2:T(8,128)S(1)}, s32[]{:T(128)}, s32[]{:T(128)}) %tuple.404), condition=%wide.region_9.10_spmd.clone.clone, body=%wide.region_7.9_spmd.clone.clone.sunk | while | flops 345459 | bytes 1228033 | solution.py:118
  519.8 11.4 %while.139 = (s32[]{:T(128)}, f32[16,2,16,128]{3,2,1,0:T(8,128)S(1)}, f32[16,2,16,128]{3,0,1,2:T(8,128)S(1)}, s32[]{:T(128)}, s32[]{:T(128)}) while((s32[]{:T(128)}, f32[16,2,16,128]{3,2,1,0:T(8,128)S(1)}, f32[16,2,16,128]{3,0,1,2:T(8,128)S(1)}, s32[]{:T(128)}, s32[]{:T(128)}) %tuple.407), condition=%wide.region_12.13_spmd.clone.clone, body=%wide.region_10.12_spmd.clone.clone.sunk | while | flops 345459 | bytes 1228033 | solution.py:118
  534.6 11.2 %while.140 = (s32[]{:T(128)}, f32[16,2,16,128]{3,2,1,0:T(8,128)S(1)}, f32[16,2,16,128]{3,0,1,2:T(8,128)S(1)}, s32[]{:T(128)}, s32[]{:T(128)}) while((s32[]{:T(128)}, f32[16,2,16,128]{3,2,1,0:T(8,128)S(1)}, f32[16,2,16,128]{3,0,1,2:T(8,128)S(1)}, s32[]{:T(128)}, s32[]{:T(128)}) %tuple.410), condition=%wide.region_15.16_spmd.clone.clone, body=%wide.region_13.15_spmd.clone.clone.sunk | while | flops 345459 | bytes 1228033 | solution.py:118
  548.5 11.2 %while.141 = (s32[]{:T(128)}, f32[16,2,16,128]{3,2,1,0:T(8,128)S(1)}, f32[16,2,16,128]{3,0,1,2:T(8,128)S(1)}, s32[]{:T(128)}, s32[]{:T(128)}) while((s32[]{:T(128)}, f32[16,2,16,128]{3,2,1,0:T(8,128)S(1)}, f32[16,2,16,128]{3,0,1,2:T(8,128)S(1)}, s32[]{:T(128)}, s32[]{:T(128)}) %tuple.413), condition=%wide.region_18.19_spmd.clone.clone, body=%wide.region_16.18_spmd.clone.clone.sunk | while | flops 345459 | bytes 1228033 | solution.py:118
  562.2 11.2 %while.142 = (s32[]{:T(128)}, f32[16,2,16,128]{3,2,1,0:T(8,128)S(1)}, f32[16,2,16,128]{3,0,1,2:T(8,128)S(1)}, s32[]{:T(128)}, s32[]{:T(128)}) while((s32[]{:T(128)}, f32[16,2,16,128]{3,2,1,0:T(8,128)S(1)}, f32[16,2,16,128]{3,0,1,2:T(8,128)S(1)}, s32[]{:T(128)}, s32[]{:T(128)}) %tuple.416), condition=%wide.region_21.22_spmd.clone.clone, body=%wide.region_19.21_spmd.clone.clone.sunk | while | flops 345459 | bytes 1228033 | solution.py:118
  577.2 11.2 %while.143 = (s32[]{:T(128)}, f32[16,2,16,128]{3,2,1,0:T(8,128)S(1)}, f32[16,2,16,128]{3,0,1,2:T(8,128)S(1)}, s32[]{:T(128)}, s32[]{:T(128)}) while((s32[]{:T(128)}, f32[16,2,16,128]{3,2,1,0:T(8,128)S(1)}, f32[16,2,16,128]{3,0,1,2:T(8,128)S(1)}, s32[]{:T(128)}, s32[]{:T(128)}) %tuple.419), condition=%wide.region_24.25_spmd.clone.clone, body=%wide.region_22.24_spmd.clone.clone.sunk | while | flops 345459 | bytes 1228033 | solution.py:118
  589.6 4.3 stack.249
  593.9 5.7 all-to-all-start.1
  599.6 4.0 copy.324
  605.9 86.8 %all-to-all-done.1 = f32[4,16,2,128,128]{4,3,2,1,0:T(8,128)} async-done(((f32[4,16,2,128,128]{4,3,2,1,0:T(8,128)}), f32[4,16,2,128,128]{4,3,2,1,0:T(8,128)}, u32[]{:S(2)}, u32[]{:S(2)}) %all-to-all-start.1) | async-done | bytes 8388640 | tf_op jit(solution)/shard_map/all_to_all | solution.py:157
  692.7 7.9 %copy.432 = f32[64,2,128,128]{3,2,1,0:T(8,128)} copy(f32[64,2,128,128]{3,2,1,0:T(8,128)} %bitcast.60) | data formatting | bytes 16777216
  (1739 shorter events, 136.3 us)
Async XLA Ops:
  7.2 458.7 %reduce-scatter.5.cloned.1.call-start = ((), (), s32[]{:S(2)}) async-start(), calls=%async_computation.3 | async-start | bytes 10485760
  15.9 6.1 copy-start.9
  20.7 9.4 %collective-permute-start = (f32[2,8,512,128]{2,3,1,0:T(8,128)}, f32[2,8,512,128]{2,3,1,0:T(8,128)}, u32[]{:S(2)}, u32[]{:S(2)}) collective-permute-start(f32[2,8,512,128]{2,3,1,0:T(8,128)} %slice.757), channel_id=1, source_target_pairs={{8,0},{16,8},{24,16},{9,1},{17,9},{25,17},{10,2},{18,10},{26,18},{... | collective-permute-start | bytes 12582920 | tf_op jit(solution)/shard_map/ppermute | solution.py:14
  22.6 13.7 %copy-start.8 = (f32[2,32896]{1,0:T(2,128)}, f32[2,32896]{1,0:T(2,128)S(1)}, u32[]{:S(2)}) copy-start(f32[2,32896]{1,0:T(2,128)S(1)} %tile.10) | copy-start | bytes 789508
  52.1 8.8 %slice-start = ((f32[2,32896]{1,0:T(2,128)}), f32[2,32768]{1,0:T(2,128)S(1)}, s32[]{:S(2)}) async-start(f32[2,32896]{1,0:T(2,128)} %copy-done.8), calls=%async_computation.4 | async-start | bytes 524288 | tf_op jit(solution)/shard_map/slice | solution.py:27
  319.1 3.5 copy-start
  319.1 9.9 %copy-start.10 = (s32[64,2]{0,1:T(2,128)S(1)}, s32[64,2]{0,1:T(2,128)}, u32[]{:S(2)}) copy-start(s32[64,2]{0,1:T(2,128)} %param.21) | copy-start | bytes 1540
  322.6 3.3 copy-start.1
  325.9 11.0 %collective-permute-start.1 = (f32[2,1,64,256]{3,2,0,1:T(8,128)S(1)}, f32[2,1,64,256]{3,2,0,1:T(8,128)S(1)}, u32[]{:S(2)}, u32[]{:S(2)}) collective-permute-start(f32[2,1,64,256]{3,2,0,1:T(8,128)S(1)} %slice.769), channel_id=1, source_target_pairs={{1,0},{2,1},{3,2},{4,3},{5,4},{6,5},{7,6},{0,7},{9,8},{10,9},{11,1... | collective-permute-start | bytes 393224 | tf_op jit(solution)/shard_map/ppermute | solution.py:20
  480.1 4.5 copy-start.2
  503.7 1.2 copy-start.3
  516.1 3.5 copy-start.4
  548.4 11.4 %copy-start.5 = (f32[16,2,128,128]{3,0,1,2:T(8,128)S(1)}, f32[16,2,128,128]{3,0,1,2:T(8,128)}, u32[]{:S(2)}) copy-start(f32[16,2,128,128]{3,0,1,2:T(8,128)} %constant_dynamic-update-slice_fusion.3) | copy-start | bytes 6291460
  561.4 0.8 copy-start.6
  562.2 14.9 %copy-start.7 = (f32[16,2,32,128]{3,2,0,1:T(8,128)S(1)}, f32[16,2,32,128]{3,2,0,1:T(8,128)}, u32[]{:S(2)}) copy-start(f32[16,2,32,128]{3,2,0,1:T(8,128)} %copy-done.6) | copy-start | bytes 1572868
  593.9 98.8 %all-to-all-start.1 = ((f32[4,16,2,128,128]{4,3,2,1,0:T(8,128)}), f32[4,16,2,128,128]{4,3,2,1,0:T(8,128)}, u32[]{:S(2)}, u32[]{:S(2)}) async-start(f32[4,16,2,128,128]{4,3,2,1,0:T(8,128)} %stack.249), calls=%async_computation.1 | async-start | bytes 16777216 | tf_op jit(solution)/shard_map/all_to_all | solution.py:157
Sparse Core Ops, SparseCore 0:
  383.8 81.9 reduce-scatter.4
